TPU v7x, 256 devices: a whole 4x4x8 slice. The times are simulated.
256 devices in a mesh: section: 8 (over y, core), row: 32 (over z, x).
Axes of the slice: x: 4, y: 4, z: 8, core: 2. Of those that a mesh axis runs over, the one named last changes fastest.
Arguments:
- channel_rows_in: bfloat16 [1024, 32, 4096], P('row', None, 'section'), may hold values from -6 to 6
- gate_rows_in: bfloat16 [1024, 32, 4096], P('row', None, 'section'), may hold values from -6 to 6
- map_input_rows: bfloat16 [1024, 32, 256], P('row'), may hold values from -6 to 6
- step_size_input: bfloat16 [1024, 64, 32], P('row', 'section'), may hold values from -4 to 4
- channel_kernel_weight: float32 [4, 4096], P(None, 'section'), may hold values from -3 to 3
- map_kernel_weight: float32 [4, 256], replicated, may hold values from -3 to 3
- channel_conv_bias: float32 [4096], P('section'), may hold values from -3 to 3
- map_kernel_bias: float32 [256], replicated, may hold values from -3 to 3
- step_size_bias: float32 [64], P('section'), may hold values from -2 to 0
- head_decay_rate: float32 [64], P('section'), may hold values from 0.003 to 1
- head_skip_weight: float32 [64], P('section'), may hold values from 0.5 to 1.5
- gated_norm_scale: float32 [4096], P('section'), may hold values from 0.5 to 1.5
- scan_state_cache: bfloat16 [1024, 64, 64, 128], P('row', 'section'), may hold values from -2 to 2
- channel_window_cache: bfloat16 [1024, 3, 4096], P('row', None, 'section'), may hold values from -6 to 6
- map_window_cache: bfloat16 [1024, 3, 256], P('row'), may hold values from -6 to 6
- adapter_down_weight: bfloat16 [32, 64, 4096], P('row', None, 'section'), may hold values from -0.09375 to 0.09375
- adapter_up_weight: bfloat16 [32, 64, 4096], P('row', None, 'section'), may hold values from -0.75 to 0.75
- session_slot_index: int32 [1024], replicated, may hold values from 0 to 1023, as said below
- lengths: int32 [1024], replicated, may hold values from 1 to 32
- session_adapter_index: int32 [1024], replicated, may hold values from 0 to 31
Outputs:
- mixer_output_rows: bfloat16 [1024, 32, 4096], P('row', None, 'section')
- adapter_delta: bfloat16 [1024, 32, 4096], P('row', None, 'section')
- scan_state_next: bfloat16 [1024, 64, 64, 128], P('row', 'section')
- channel_window_next: bfloat16 [1024, 3, 4096], P('row', None, 'section')
- map_window_next: bfloat16 [1024, 3, 256], P('row')
Inputs may be any that keep to these rules, and one draw needn't show every extreme that they name: `session_slot_index`: A permutation of the 1024 cache slots; cache slot c lies on row c // 32 and served session q on row q // 32. The states of one serving row's sessions come from exactly 16 home rows, 2 from each, so every home row also sends to that many rows.
All inputs are finite; a program needn't handle non-finite values.
Results may differ from a plain program's by a relative error of at most 0.0058.
Values may be sent and summed in bfloat16 or wider, within the bound.
No kernel may reach another device: no remote copies, remote signals or barrier semaphores. Data moves between devices by JAX's collectives and lax.ppermute only.
A program may use at most 128 MiB of HBM per device.

v0:
```python
import jax
import jax.numpy as jnp
from jax import lax
from jax.sharding import PartitionSpec as P

INNER_CHANNELS = 4096


NORM_EPS = 1e-05


def sigmoid_linear(value):
    return value / (1.0 + jnp.exp(-value))


def conv_part(cached, fresh, weight, offset):
    extended = jnp.concatenate([cached.astype(jnp.float32), fresh.astype(jnp.float32)], axis=1)
    span_len = fresh.shape[1]
    summed = (
        offset + weight[0] * extended[:, 0:span_len] + weight[1] * extended[:, 1 : span_len + 1]
    )
    summed = (
        summed
        + weight[2] * extended[:, 2 : span_len + 2]
        + weight[3] * extended[:, 3 : span_len + 3]
    )
    return (sigmoid_linear(summed), extended)


def tail_state(extended, lengths):
    total_rows = extended.shape[1]
    picked = lengths[:, None] + jnp.arange(3, dtype=jnp.int32)[None, :]
    onehot = (picked[:, :, None] == jnp.arange(total_rows, dtype=jnp.int32)[None, None, :]).astype(
        jnp.float32
    )
    return jnp.einsum("skt,stc->skc", onehot, extended, precision=lax.Precision.HIGHEST).astype(
        jnp.bfloat16
    )


def mix_sessions(
    channel_rows_in,
    map_input_rows,
    step_size_input,
    lengths,
    scan_state_cache,
    channel_window_cache,
    map_window_cache,
    channel_kernel_weight,
    map_kernel_weight,
    channel_conv_bias,
    map_kernel_bias,
    step_size_bias,
    head_decay_rate,
    head_skip_weight,
):
    highest = lax.Precision.HIGHEST
    local_sess, span_len, channels = channel_rows_in.shape
    head_count = step_size_input.shape[1]
    head_dim = channels // head_count
    state_dim = map_input_rows.shape[2] // 2
    conv_x, ext_x = conv_part(
        channel_window_cache, channel_rows_in, channel_kernel_weight, channel_conv_bias
    )
    conv_m, ext_m = conv_part(map_window_cache, map_input_rows, map_kernel_weight, map_kernel_bias)
    valid = (jnp.arange(span_len, dtype=jnp.int32)[None, :] < lengths[:, None]).astype(jnp.float32)
    step_size = (
        jax.nn.softplus(step_size_input.astype(jnp.float32) + step_size_bias[None, :, None])
        * valid[:, None, :]
    )
    log_decay = jnp.cumsum(-head_decay_rate[None, :, None] * step_size, axis=2)
    input_map = conv_m[:, :, :state_dim]
    output_map = conv_m[:, :, state_dim:]
    x_heads = conv_x.reshape(local_sess, span_len, head_count, head_dim)
    per_block = max(1, 128 // span_len)
    block_count = local_sess // per_block
    block_rows = per_block * span_len
    owners = jnp.arange(block_rows) // span_len
    position = jnp.arange(block_rows)
    causal_mask = (owners[:, None] == owners[None, :]) & (position[:, None] >= position[None, :])
    decay_rows = jnp.transpose(log_decay, (0, 2, 1)).reshape(block_count, block_rows, head_count)
    decay_heads = jnp.transpose(decay_rows, (0, 2, 1))
    spread = decay_heads[:, :, :, None] - decay_heads[:, :, None, :]
    decay_mat = jnp.where(causal_mask, jnp.exp(jnp.where(causal_mask, spread, 0.0)), 0.0)
    in_rows = input_map.reshape(block_count, block_rows, state_dim)
    out_rows = output_map.reshape(block_count, block_rows, state_dim)
    scores = jnp.einsum("btn,bun->btu", out_rows, in_rows, precision=highest)
    step_rows = jnp.transpose(step_size, (0, 2, 1)).reshape(block_count, block_rows, head_count)
    scaled_x = (
        x_heads.reshape(block_count, block_rows, head_count, head_dim) * step_rows[:, :, :, None]
    )
    inside = jnp.einsum("bhtu,buhp->bthp", decay_mat * scores[:, None], scaled_x, precision=highest)
    inside = inside.reshape(local_sess, span_len, head_count, head_dim)
    state_old = scan_state_cache.astype(jnp.float32)
    carried = jnp.einsum("stn,shpn->sthp", output_map, state_old, precision=highest)
    carried = carried * jnp.exp(jnp.transpose(log_decay, (0, 2, 1)))[:, :, :, None]
    mixed_out = (inside + carried + head_skip_weight[None, None, :, None] * x_heads) * valid[
        :, :, None, None
    ]
    final_log = log_decay[:, :, -1]
    weights = jnp.exp(final_log[:, :, None] - log_decay) * step_size
    state_new = jnp.exp(final_log)[:, :, None, None] * state_old
    state_new = state_new + jnp.einsum(
        "sht,sthp,stn->shpn", weights, x_heads, input_map, precision=highest
    )
    return (
        mixed_out.reshape(local_sess, span_len, channels),
        state_new.astype(jnp.bfloat16),
        tail_state(ext_x, lengths),
        tail_state(ext_m, lengths),
    )


def pick_rows(source_rows, take_index, used_mask):
    row_total = source_rows.shape[0]
    onehot = (take_index[:, None] == jnp.arange(row_total, dtype=jnp.int32)[None, :]) & used_mask[
        :, None
    ]
    picked = jnp.dot(
        onehot.astype(source_rows.dtype),
        source_rows,
        preferred_element_type=jnp.float32,
        precision=lax.Precision.HIGHEST,
    )
    return picked.astype(source_rows.dtype)


def select_rows(source_rows, take_index):
    return pick_rows(source_rows, take_index, jnp.ones(take_index.shape, jnp.bool_))


def shards(
    channel_rows_in,
    gate_rows_in,
    map_input_rows,
    step_size_input,
    channel_kernel_weight,
    map_kernel_weight,
    channel_conv_bias,
    map_kernel_bias,
    step_size_bias,
    head_decay_rate,
    head_skip_weight,
    gated_norm_scale,
    scan_state_cache,
    channel_window_cache,
    map_window_cache,
    adapter_down_weight,
    adapter_up_weight,
    session_slot_index,
    lengths,
    session_adapter_index,
):
    local_sess = channel_rows_in.shape[0]
    row_count = lax.axis_size("row")
    row_index = lax.axis_index("row")
    capacity = max(2, 2 * local_sess // row_count)
    slot_count = row_count * capacity
    home_rows = (session_slot_index // local_sess).reshape(row_count, local_sess)
    same_home = home_rows[:, :, None] == home_rows[:, None, :]
    earlier = jnp.arange(local_sess)[None, :] < jnp.arange(local_sess)[:, None]
    rank_in_pair = (
        jnp.sum(jnp.where(same_home & earlier[None], 1, 0), axis=2).astype(jnp.int32).reshape(-1)
    )
    serve_rows = jnp.arange(row_count * local_sess, dtype=jnp.int32) // local_sess
    target = serve_rows * capacity + rank_in_pair
    source = session_slot_index // local_sess * capacity + rank_in_pair
    serve_slots = lax.dynamic_slice_in_dim(source, row_index * local_sess, local_sess)
    serve_lengths = lax.dynamic_slice_in_dim(lengths, row_index * local_sess, local_sess)
    serve_adapter = lax.dynamic_slice_in_dim(
        session_adapter_index, row_index * local_sess, local_sess
    )
    local_cache = jnp.arange(local_sess, dtype=jnp.int32) + row_index * local_sess
    cache_match = session_slot_index[None, :] == local_cache[:, None]
    home_slots = jnp.sum(jnp.where(cache_match, target[None, :], 0), axis=1)
    slot_range = jnp.arange(slot_count, dtype=jnp.int32)[:, None]
    local_range = jnp.arange(local_sess, dtype=jnp.int32)[None, :]
    home_fill = slot_range == home_slots[None, :]
    home_take = jnp.sum(jnp.where(home_fill, local_range, 0), axis=1)
    home_used = jnp.any(home_fill, axis=1)
    serve_fill = slot_range == serve_slots[None, :]
    serve_take = jnp.sum(jnp.where(serve_fill, local_range, 0), axis=1)
    serve_used = jnp.any(serve_fill, axis=1)
    layer_params = (
        channel_kernel_weight,
        map_kernel_weight,
        channel_conv_bias,
        map_kernel_bias,
        step_size_bias,
        head_decay_rate,
        head_skip_weight,
    )
    received = (
        lax.all_to_all(
            pick_rows(scan_state_cache.reshape(local_sess, -1), home_take, home_used),
            "row",
            split_axis=0,
            concat_axis=0,
            tiled=True,
        ),
        lax.all_to_all(
            pick_rows(channel_window_cache.reshape(local_sess, -1), home_take, home_used),
            "row",
            split_axis=0,
            concat_axis=0,
            tiled=True,
        ),
        lax.all_to_all(
            pick_rows(map_window_cache.reshape(local_sess, -1), home_take, home_used),
            "row",
            split_axis=0,
            concat_axis=0,
            tiled=True,
        ),
    )
    state_here = select_rows(received[0], serve_slots).reshape(scan_state_cache.shape)
    conv_here = select_rows(received[1], serve_slots).reshape(channel_window_cache.shape)
    map_here = select_rows(received[2], serve_slots).reshape(map_window_cache.shape)
    mixed, state_new, conv_new, map_new = mix_sessions(
        channel_rows_in,
        map_input_rows,
        step_size_input,
        serve_lengths,
        state_here,
        conv_here,
        map_here,
        *layer_params
    )
    returned = (
        lax.all_to_all(
            pick_rows(state_new.reshape(local_sess, -1), serve_take, serve_used),
            "row",
            split_axis=0,
            concat_axis=0,
            tiled=True,
        ),
        lax.all_to_all(
            pick_rows(conv_new.reshape(local_sess, -1), serve_take, serve_used),
            "row",
            split_axis=0,
            concat_axis=0,
            tiled=True,
        ),
        lax.all_to_all(
            pick_rows(map_new.reshape(local_sess, -1), serve_take, serve_used),
            "row",
            split_axis=0,
            concat_axis=0,
            tiled=True,
        ),
    )
    scan_state_next = select_rows(returned[0], home_slots).reshape(scan_state_cache.shape)
    channel_window_next = select_rows(returned[1], home_slots).reshape(channel_window_cache.shape)
    map_window_next = select_rows(returned[2], home_slots).reshape(map_window_cache.shape)
    gated = mixed * sigmoid_linear(gate_rows_in.astype(jnp.float32))
    square_sum = lax.psum(jnp.sum(gated * gated, axis=2), "section")
    inv_rms = lax.rsqrt(square_sum / INNER_CHANNELS + NORM_EPS)
    mixer_output_rows = (gated * inv_rms[:, :, None] * gated_norm_scale).astype(jnp.bfloat16)
    pieces = (
        lax.all_gather(adapter_down_weight, "row", axis=0, tiled=True),
        lax.all_gather(adapter_up_weight, "row", axis=0, tiled=True),
    )
    piece_len = pieces[0].shape[0]
    chosen = (serve_adapter[:, None] == jnp.arange(piece_len, dtype=jnp.int32)[None, :]).astype(
        jnp.bfloat16
    )
    down_part = jnp.einsum("sk,krc->src", chosen, pieces[0], preferred_element_type=jnp.float32)
    up_part = jnp.einsum("sk,krc->src", chosen, pieces[1], preferred_element_type=jnp.float32)
    low_part = jnp.einsum(
        "std,srd->str",
        mixer_output_rows,
        down_part.astype(jnp.bfloat16),
        preferred_element_type=jnp.float32,
    )
    low_total = lax.psum(low_part, "section").astype(jnp.bfloat16)
    adapter_delta = jnp.einsum(
        "str,src->stc", low_total, up_part.astype(jnp.bfloat16), preferred_element_type=jnp.float32
    ).astype(jnp.bfloat16)
    return (mixer_output_rows, adapter_delta, scan_state_next, channel_window_next, map_window_next)


def solution(mesh):
    return jax.shard_map(
        shards,
        mesh=mesh,
        in_specs=(
            P("row", None, "section"),
            P("row", None, "section"),
            P("row", None, None),
            P("row", "section", None),
            P(None, "section"),
            P(),
            P("section"),
            P(),
            P("section"),
            P("section"),
            P("section"),
            P("section"),
            P("row", "section", None, None),
            P("row", None, "section"),
            P("row", None, None),
            P("row", None, "section"),
            P("row", None, "section"),
            P(),
            P(),
            P(),
        ),
        out_specs=(
            P("row", None, "section"),
            P("row", None, "section"),
            P("row", "section", None, None),
            P("row", None, "section"),
            P("row", None, None),
        ),
        check_vma=False,
    )
```

profile of v0, /device:TPU:2, one launch (start us, length us, event | category | flops | bytes accessed | tf_op | source)
XLA Modules:
  0.0 663.2 jit_solution(1876397155071708182)
XLA Ops:
  12.7 11.6 %all-to-all-start.1 = ((bf16[32,2,768]{2,1,0:T(2,128)(2,1)}), bf16[32,2,768]{2,1,0:T(2,128)(2,1)S(1)}, u32[]{:S(2)}, u32[]{:S(2)}) async-start(bf16[32,2,768]{2,1,0:T(2,128)(2,1)} %all_to_all.51), calls=%async_computation.1 | async-start | bytes 196608 | tf_op jit(solution)/shard_map/all_to_all | solution.py:208
  26.2 6.9 %all-to-all-done.1 = bf16[32,2,768]{2,1,0:T(2,128)(2,1)S(1)} async-done(((bf16[32,2,768]{2,1,0:T(2,128)(2,1)}), bf16[32,2,768]{2,1,0:T(2,128)(2,1)S(1)}, u32[]{:S(2)}, u32[]{:S(2)}) %all-to-all-start.1) | async-done | bytes 98336 | tf_op jit(solution)/shard_map/all_to_all | solution.py:208
  33.1 5.2 all-to-all-start
  38.3 8.3 %convolution_convert_fusion.1 = bf16[64,65536]{1,0:T(8,128)(2,1)} fusion(bf16[4,8,512,128]{3,2,1,0:T(8,128)(2,1)} %bitcast.95, s32[64]{0:T(128)S(1)} %select_reduce_fusion.3, pred[64]{0:T(512)(128)(4,1)S(1)} %fusion.97), kind=kOutput, calls=%fused_computation.1 | convolution fusion | flops 272633856 | bytes 12583232 | tf_op jit(solution)/shard_map/dot_general | solution.py:119
  46.6 10.5 %all_to_all.54 = bf16[32,2,65536]{2,1,0:T(2,128)(2,1)} reshape(bf16[64,65536]{1,0:T(8,128)(2,1)} %convolution_convert_fusion.1) | data formatting | bytes 16777216 | tf_op jit(solution)/shard_map/all_to_all | solution.py:194
  57.2 10.8 %all-to-all-start.2 = ((bf16[32,2,65536]{2,1,0:T(2,128)(2,1)}), bf16[32,2,65536]{2,1,0:T(2,128)(2,1)}, u32[]{:S(2)}, u32[]{:S(2)}) async-start(bf16[32,2,65536]{2,1,0:T(2,128)(2,1)} %all_to_all.54), calls=%async_computation.2 | async-start | bytes 16777216 | tf_op jit(solution)/shard_map/all_to_all | solution.py:194
  69.1 5.9 reduce_window_sum.11
  99.8 149.5 %all-to-all-done.2 = bf16[32,2,65536]{2,1,0:T(2,128)(2,1)} async-done(((bf16[32,2,65536]{2,1,0:T(2,128)(2,1)}), bf16[32,2,65536]{2,1,0:T(2,128)(2,1)}, u32[]{:S(2)}, u32[]{:S(2)}) %all-to-all-start.2) | async-done | bytes 8388640 | tf_op jit(solution)/shard_map/all_to_all | solution.py:194
  249.3 13.7 %all-to-all-start.5 = ((bf16[32,2,768]{2,1,0:T(2,128)(2,1)}), bf16[32,2,768]{2,1,0:T(2,128)(2,1)S(1)}, u32[]{:S(2)}, u32[]{:S(2)}) async-start(bf16[32,2,768]{2,1,0:T(2,128)(2,1)} %all_to_all.63), calls=%async_computation.5 | async-start | bytes 196608 | tf_op jit(solution)/shard_map/all_to_all | solution.py:244
  263.0 10.2 %all_to_all.56 = bf16[64,65536]{1,0:T(8,128)(2,1)} reshape(bf16[32,2,65536]{2,1,0:T(2,128)(2,1)} %all-to-all-done.2) | data formatting | bytes 16777216 | tf_op jit(solution)/shard_map/all_to_all | solution.py:194
  280.9 15.8 %add_convert_fusion = bf16[32,8,64,128]{3,2,1,0:T(8,128)(2,1)} fusion(bf16[32,8,64,128]{3,2,1,0:T(8,128)(2,1)S(1)} %bitcast.91, f32[32,8]{1,0:T(8,128)S(1)} %copy-done.15, f32[32,32,8,64]{3,2,1,0:T(8,128)S(1)} %copy-done.2, f32[32,32,256]{2,1,0:T(8,128)S(1)} %add_divide_fusion.1), kind=kOutput, calls=%fused_computation.4 | convolution fusion | flops 813694976 | bytes 13123584 | tf_op jit(solution)/shard_map/sht,sthp,stn->shpn/dot_general | solution.py:103
  297.3 9.8 %all-to-all-start.4 = ((bf16[32,2,1536]{2,1,0:T(2,128)(2,1)}), bf16[32,2,1536]{2,1,0:T(2,128)(2,1)S(1)}, u32[]{:S(2)}, u32[]{:S(2)}) async-start(bf16[32,2,1536]{2,1,0:T(2,128)(2,1)} %all_to_all.60), calls=%async_computation.4 | async-start | bytes 393216 | tf_op jit(solution)/shard_map/all_to_all | solution.py:237
  307.1 8.3 %convolution_convert_fusion = bf16[64,65536]{1,0:T(8,128)(2,1)} fusion(bf16[4,8,512,128]{3,2,1,0:T(8,128)(2,1)} %bitcast.93, s32[64]{0:T(128)S(1)} %copy-done.20, pred[64]{0:T(512)(128)(4,1)S(1)} %copy-done.22), kind=kOutput, calls=%fused_computation | convolution fusion | flops 272633856 | bytes 12583232 | tf_op jit(solution)/shard_map/dot_general | solution.py:119
  315.4 10.5 %all_to_all.57 = bf16[32,2,65536]{2,1,0:T(2,128)(2,1)} reshape(bf16[64,65536]{1,0:T(8,128)(2,1)} %convolution_convert_fusion) | data formatting | bytes 16777216 | tf_op jit(solution)/shard_map/all_to_all | solution.py:230
  326.0 9.8 %all-to-all-start.3 = ((bf16[32,2,65536]{2,1,0:T(2,128)(2,1)}), bf16[32,2,65536]{2,1,0:T(2,128)(2,1)}, u32[]{:S(2)}, u32[]{:S(2)}) async-start(bf16[32,2,65536]{2,1,0:T(2,128)(2,1)} %all_to_all.57), calls=%async_computation.3 | async-start | bytes 16777216 | tf_op jit(solution)/shard_map/all_to_all | solution.py:230
  351.3 8.9 %fusion.53 = f32[8,128,8,64]{1,3,2,0:T(8,128)S(1)} fusion(f32[8,128,128]{2,1,0:T(8,128)S(1)} %copy-done.10, f32[8,8,128]{2,1,0:T(8,128)S(1)} %copy.74, pred[128,128]{1,0:T(8,128)(4,1)S(1)} %fusion.79, f32[8,128,8,64]{3,2,1,0:T(8,128)S(1)} %broadcast_multiply_fusion.1), kind=kOutput, calls=%fused_computation.76 | convolution fusion | flops 809500672 | bytes 4767744 | tf_op jit(solution)/shard_map/bhtu,buhp->bthp/dot_general | solution.py:92
  365.0 82.9 %all-gather.5.cloned.1.call-done = bf16[32,64,512]{2,1,0:T(8,128)(2,1)} async-done(((bf16[1,64,512]{2,1,0:T(8,128)(2,1)}), bf16[32,64,512]{2,1,0:T(8,128)(2,1)}) %all-gather.5.cloned.1.call-update) | async-done | bytes 2097168 | tf_op jit(solution)/shard_map/all_gather | solution.py:261
  452.5 97.4 %all-gather.3.cloned.1.call-done = bf16[32,64,512]{2,1,0:T(8,128)(2,1)} async-done(((bf16[1,64,512]{2,1,0:T(8,128)(2,1)}), bf16[32,64,512]{2,1,0:T(8,128)(2,1)}) %all-gather.3.cloned.1.call-update) | async-done | bytes 2097168 | tf_op jit(solution)/shard_map/all_gather | solution.py:260
  549.9 4.8 fusion.47
  554.7 13.9 %fusion.7 = f32[32,32,8,64]{3,1,2,0:T(8,128)S(1)} fusion(f32[32,32,8,64]{3,2,1,0:T(8,128)S(1)} %copy-done, f32[32,32,8,64]{3,2,1,0:T(8,128)} %bitcast.94, bf16[32,8,64,128]{3,2,1,0:T(8,128)(2,1)} %bitcast.92, f32[32,32]{1,0:T(8,128)S(1)} %fusion.104, f32[8]{0:T(128)S(1)} %copy-done.30, f32[32,32,8]{1,2,0:T(8,128)S(1)} %copy-done.8, ...), kind=kOutput, calls=%fused_computation.17 | convolution fusion | flops 807927808 | bytes 13255168 | tf_op jit(solution)/shard_map/stn,shpn->sthp/dot_general | solution.py:95
  568.6 5.8 copy.81
  578.7 23.9 %psum.14 = f32[32,32]{1,0:T(8,128)S(1)} all-reduce(f32[32,32]{1,0:T(8,128)S(1)} %multiply_reduce_fusion), channel_id=1, replica_groups=mesh['section'=8,'row'=32] {'section'}, use_global_device_ids=true, to_apply=%region_6.7 | all-reduce | flops 1024 | bytes 8192 | tf_op jit(solution)/shard_map/psum | solution.py:256
  605.6 29.2 %all-reduce.1 = bf16[32,32,64]{2,1,0:T(8,128)(2,1)S(1)} all-reduce(f32[32,32,64]{2,1,0:T(8,128)S(1)} %fusion.38), channel_id=1, replica_groups=mesh['section'=8,'row'=32] {'section'}, use_global_device_ids=true, to_apply=%region_7.8 | all-reduce | flops 65536 | bytes 393216 | tf_op jit(solution)/shard_map/psum | solution.py:275
  638.3 10.2 %all_to_all.59 = bf16[64,65536]{1,0:T(8,128)(2,1)} reshape(bf16[32,2,65536]{2,1,0:T(2,128)(2,1)} %all-to-all-done.3) | data formatting | bytes 16777216 | tf_op jit(solution)/shard_map/all_to_all | solution.py:230
  (155 shorter events, 84.6 us)
Async XLA Ops:
  12.7 20.4 %all-to-all-start.1 = ((bf16[32,2,768]{2,1,0:T(2,128)(2,1)}), bf16[32,2,768]{2,1,0:T(2,128)(2,1)S(1)}, u32[]{:S(2)}, u32[]{:S(2)}) async-start(bf16[32,2,768]{2,1,0:T(2,128)(2,1)} %all_to_all.51), calls=%async_computation.1 | async-start | bytes 196608 | tf_op jit(solution)/shard_map/all_to_all | solution.py:208
  33.1 24.1 %all-to-all-start = ((bf16[32,2,1536]{2,1,0:T(2,128)(2,1)}), bf16[32,2,1536]{2,1,0:T(2,128)(2,1)S(1)}, u32[]{:S(2)}, u32[]{:S(2)}) async-start(bf16[32,2,1536]{2,1,0:T(2,128)(2,1)} %all_to_all.48), calls=%async_computation | async-start | bytes 393216 | tf_op jit(solution)/shard_map/all_to_all | solution.py:201
  57.2 10.9 %copy-start.31 = (f32[8]{0:T(128)S(1)}, f32[8]{0:T(128)}, u32[]{:S(2)}) copy-start(f32[8]{0:T(128)} %param.29) | copy-start | bytes 100
  57.2 11.8 %copy-start.13 = (bf16[32,8,32]{2,1,0:T(8,128)(2,1)S(1)}, bf16[32,8,32]{2,1,0:T(8,128)(2,1)}, u32[]{:S(2)}) copy-start(bf16[32,8,32]{2,1,0:T(8,128)(2,1)} %param.23) | copy-start | bytes 49156
  57.2 11.8 %copy-start.27 = (f32[8]{0:T(128)S(1)}, f32[8]{0:T(128)}, u32[]{:S(2)}) copy-start(f32[8]{0:T(128)} %param.28) | copy-start | bytes 100
  57.2 18.3 %copy-start.7 = (bf16[32,32,512]{2,1,0:T(8,128)(2,1)S(1)}, bf16[32,32,512]{2,1,0:T(8,128)(2,1)}, u32[]{:S(2)}) copy-start(bf16[32,32,512]{2,1,0:T(8,128)(2,1)} %param.20) | copy-start | bytes 3145732
  57.2 192.1 %all-to-all-start.2 = ((bf16[32,2,65536]{2,1,0:T(2,128)(2,1)}), bf16[32,2,65536]{2,1,0:T(2,128)(2,1)}, u32[]{:S(2)}, u32[]{:S(2)}) async-start(bf16[32,2,65536]{2,1,0:T(2,128)(2,1)} %all_to_all.54), calls=%async_computation.2 | async-start | bytes 16777216 | tf_op jit(solution)/shard_map/all_to_all | solution.py:194
  68.0 9.2 %copy-start.9 = (bf16[32,32,256]{2,1,0:T(8,128)(2,1)S(1)}, bf16[32,32,256]{2,1,0:T(8,128)(2,1)}, u32[]{:S(2)}) copy-start(bf16[32,32,256]{2,1,0:T(8,128)(2,1)} %param.22) | copy-start | bytes 1572868
  68.0 12.1 %copy-start.25 = (f32[4,256]{1,0:T(4,128)S(1)}, f32[4,256]{1,0:T(4,128)}, u32[]{:S(2)}) copy-start(f32[4,256]{1,0:T(4,128)} %param.25) | copy-start | bytes 12292
  68.0 12.1 %copy-start.18 = (f32[4,512]{1,0:T(4,128)S(1)}, f32[4,512]{1,0:T(4,128)}, u32[]{:S(2)}) copy-start(f32[4,512]{1,0:T(4,128)} %param.24) | copy-start | bytes 24580
  75.4 7.3 %copy-start.29 = (f32[256]{0:T(256)S(1)}, f32[256]{0:T(256)}, u32[]{:S(2)}) copy-start(f32[256]{0:T(256)} %param.27) | copy-start | bytes 3076
  249.3 47.4 %all-to-all-start.5 = ((bf16[32,2,768]{2,1,0:T(2,128)(2,1)}), bf16[32,2,768]{2,1,0:T(2,128)(2,1)S(1)}, u32[]{:S(2)}, u32[]{:S(2)}) async-start(bf16[32,2,768]{2,1,0:T(2,128)(2,1)} %all_to_all.63), calls=%async_computation.5 | async-start | bytes 196608 | tf_op jit(solution)/shard_map/all_to_all | solution.py:244
  263.0 10.2 %copy-start.24 = (s32[32]{0:T(128)S(1)}, s32[32]{0:T(128)}, u32[]{:S(2)}) copy-start(s32[32]{0:T(128)} %copy-done.23) | copy-start | bytes 388
  280.8 26.3 %copy-start.20 = (s32[64]{0:T(128)S(1)}, s32[64]{0:T(128)}, u32[]{:S(2)}) copy-start(s32[64]{0:T(128)} %copy-done.19) | copy-start | bytes 772
  280.8 26.3 %copy-start.22 = (pred[64]{0:T(512)(128)(4,1)S(1)}, pred[64]{0:T(512)(128)(4,1)}, u32[]{:S(2)}) copy-start(pred[64]{0:T(512)(128)(4,1)} %copy-done.21) | copy-start | bytes 196
  297.3 28.7 %all-to-all-start.4 = ((bf16[32,2,1536]{2,1,0:T(2,128)(2,1)}), bf16[32,2,1536]{2,1,0:T(2,128)(2,1)S(1)}, u32[]{:S(2)}, u32[]{:S(2)}) async-start(bf16[32,2,1536]{2,1,0:T(2,128)(2,1)} %all_to_all.60), calls=%async_computation.4 | async-start | bytes 393216 | tf_op jit(solution)/shard_map/all_to_all | solution.py:237
  326.0 312.4 %all-to-all-start.3 = ((bf16[32,2,65536]{2,1,0:T(2,128)(2,1)}), bf16[32,2,65536]{2,1,0:T(2,128)(2,1)}, u32[]{:S(2)}, u32[]{:S(2)}) async-start(bf16[32,2,65536]{2,1,0:T(2,128)(2,1)} %all_to_all.57), calls=%async_computation.3 | async-start | bytes 16777216 | tf_op jit(solution)/shard_map/all_to_all | solution.py:230
  335.8 112.1 %all-gather.5.cloned.1.call-start = ((), (), s32[]{:S(2)}) async-start(), calls=%async_computation.7 | async-start | bytes 2162688 | tf_op jit(solution)/shard_map/all_gather | solution.py:261
  336.6 213.3 %all-gather.3.cloned.1.call-start = ((), (), s32[]{:S(2)}) async-start(), calls=%async_computation.6 | async-start | bytes 2162688 | tf_op jit(solution)/shard_map/all_gather | solution.py:260
  360.2 87.7 %copy-start.28 = (s32[32]{0:T(128)S(1)}, s32[32]{0:T(128)}, u32[]{:S(2)}) copy-start(s32[32]{0:T(128)} %dynamic_slice.11) | copy-start | bytes 388
  365.0 189.7 %copy-start.8 = (f32[32,32,8]{1,2,0:T(8,128)S(1)}, f32[32,32,8]{1,2,0:T(8,128)}, u32[]{:S(2)}) copy-start(f32[32,32,8]{1,2,0:T(8,128)} %bitcast_exponential_fusion.1) | copy-start | bytes 98308
  365.0 189.7 %copy-start.30 = (f32[8]{0:T(128)S(1)}, f32[8]{0:T(128)}, u32[]{:S(2)}) copy-start(f32[8]{0:T(128)} %param.30) | copy-start | bytes 100
  574.4 28.2 %copy-start.26 = (f32[512]{0:T(512)S(1)}, f32[512]{0:T(512)}, u32[]{:S(2)}) copy-start(f32[512]{0:T(512)} %param.31) | copy-start | bytes 6148
  604.3 30.4 %copy-start.4 = (bf16[32,64,512]{2,0,1:T(8,128)(2,1)S(1)}, bf16[32,64,512]{2,0,1:T(8,128)(2,1)}, u32[]{:S(2)}) copy-start(bf16[32,64,512]{2,0,1:T(8,128)(2,1)} %fusion.50) | copy-start | bytes 6291460
  (16 other events, 44.4 us)
Sparse Core Ops, SparseCore 0:
  339.2 108.6 all-gather.4
  450.5 99.3 all-gather.2
where the time goes:
time: 670 us; the launch traced here: 663 us
  waiting for transfers between devices  338 us (50%)
  matrix products  86.7 us (13%)
  local copies, waits for them, and re-layouts  82.4 us (12%)
  starting transfers between devices  61.4 us (9%)
  blocking collectives  53 us (8%)
  other arithmetic  27.2 us (4%)
  between operations  14.9 us (2%)
    all_to_all x1, waiting for transfers between devices, shards(): lax.all_to_all(pick_rows(scan_state_cache.reshape(local_sess, -1), home_t...  149 us
    all_gather x1, waiting for transfers between devices, shards(): lax.all_gather(adapter_down_weight, 'row', axis=0, tiled=True)  97.4 us
    all_gather x1, waiting for transfers between devices, shards(): lax.all_gather(adapter_up_weight, 'row', axis=0, tiled=True)  82.9 us
    psum x1, blocking collectives, shards(): low_total = lax.psum(low_part, 'section').astype(jnp.bfloat16)  29.2 us
    dot_general x12, matrix products, pick_rows(): jnp.dot(onehot.astype(source_rows.dtype), source_rows, preferred_element_...  28.4 us
    psum x1, blocking collectives, shards(): square_sum = lax.psum(jnp.sum(gated * gated, axis=2), 'section')  23.9 us
    all_to_all x2, local copies, waits for them, and re-layouts, shards(): lax.all_to_all(pick_rows(scan_state_cache.reshape(local_sess, -1), home_t...  20.7 us
    all_to_all x2, local copies, waits for them, and re-layouts, shards(): lax.all_to_all(pick_rows(state_new.reshape(local_sess, -1), serve_take, s...  20.7 us
  transfers between devices with their start and end apart: 8, of which 4 were waited for; matrix products, arithmetic and copies ran while one was open for 20% of the time, Pallas kernels for 0%

commit v1 on v0

v1 whole, which is shorter than its diff:
```python
import jax
import jax.numpy as jnp
from jax import lax
from jax.experimental import pallas as pl
from jax.experimental.pallas import tpu as pltpu
from jax.sharding import PartitionSpec as P


NORM_EPS = 1e-05
PAIR = 2
CHUNKS = 2
GROUP = 4
BATCH = 4

F32 = jnp.float32
BF16 = jnp.bfloat16


def silu(value):
    return value / (1.0 + jnp.exp(-value))


def halves(value):
    high = value.astype(BF16)
    return high, (value - high.astype(F32)).astype(BF16)


def dot_nn(left, right):
    return lax.dot_general(left, right, (((1,), (0,)), ((), ())), preferred_element_type=F32)


def dot_nt(left, right):
    return lax.dot_general(left, right, (((1,), (1,)), ((), ())), preferred_element_type=F32)


def dot_tn(left, right):
    return lax.dot_general(left, right, (((0,), (0,)), ((), ())), preferred_element_type=F32)


def params(megabytes=62):
    return pltpu.CompilerParams(vmem_limit_bytes=megabytes * 1024 * 1024)


def cost(flops, moved, transcendentals=0):
    return pl.CostEstimate(
        flops=int(flops), bytes_accessed=int(moved), transcendentals=int(transcendentals)
    )


def convolve(ext_ref, kernel_rows, offset, tokens):
    summed = offset + kernel_rows[0:1] * ext_ref[5 : 5 + tokens]
    for tap in range(1, 4):
        summed = summed + kernel_rows[tap : tap + 1] * ext_ref[5 + tap : 5 + tap + tokens]
    return silu(summed)


def pack_small(slots, rank_here, map_slice, step_rows):
    sessions, group_tokens, width = map_slice.shape
    rows = lax.axis_size("row")

    def body(slot_ref, rank_ref, map_ref, step_ref, out_ref, held_ref):
        for q in range(sessions):
            slot = slot_ref[q]
            home = slot // PAIR
            rank = slot % PAIR
            held_ref[home, pl.ds(rank, 1), :] = step_ref[q : q + 1, :]

            @pl.when(rank == rank_ref[0])
            def _():
                out_ref[home, 0:group_tokens, :] = map_ref[q]

        out_ref[:, group_tokens:, :] = held_ref[...].astype(BF16)

    vmem = pl.BlockSpec(memory_space=pltpu.VMEM)
    smem = pl.BlockSpec(memory_space=pltpu.SMEM)
    return pl.pallas_call(
        body,
        out_shape=jax.ShapeDtypeStruct((rows, group_tokens + 8, width), BF16),
        in_specs=[smem, smem, vmem, vmem],
        out_specs=vmem,
        scratch_shapes=[pltpu.VMEM((rows, 8, width), F32)],
        compiler_params=params(),
        cost_estimate=cost(0, 1 << 20),
        name="pack_small",
    )(slots, rank_here, map_slice, step_rows)


def pack_channels(slots, rows_in, slot_total):
    sessions, tokens, channels = rows_in.shape
    width = channels // CHUNKS

    def body(slot_ref, in_ref, *rest):
        outs = rest[:CHUNKS]
        sems = rest[CHUNKS]

        def copies(q):
            slot = slot_ref[q]
            return [
                pltpu.make_async_copy(
                    in_ref.at[q, :, k * width : (k + 1) * width],
                    outs[k].at[slot],
                    sems.at[k * sessions + q],
                )
                for k in range(CHUNKS)
            ]

        for q in range(sessions):
            for copy in copies(q):
                copy.start()
        for q in range(sessions):
            for copy in copies(q):
                copy.wait()

    return pl.pallas_call(
        body,
        out_shape=[jax.ShapeDtypeStruct((slot_total, tokens, width), BF16)] * CHUNKS,
        in_specs=[
            pl.BlockSpec(memory_space=pltpu.SMEM),
            pl.BlockSpec(memory_space=pltpu.VMEM),
        ],
        out_specs=[pl.BlockSpec(memory_space=pl.ANY)] * CHUNKS,
        scratch_shapes=[pltpu.SemaphoreType.DMA((CHUNKS * sessions,))],
        compiler_params=params(),
        cost_estimate=cost(0, 4 << 20),
        name="pack_channels",
    )(slots, rows_in)


def prepare(slots, lens, lens_col, maps, small, map_window, state, map_kernel, map_bias, bias_row, decay_row):
    sessions, heads, head_dim, state_dim = state.shape
    groups, rows, group_tokens, width = maps.shape
    side = groups // PAIR
    tokens = side * group_tokens
    spread = heads * tokens
    channels = heads * head_dim
    chunk_heads = heads // CHUNKS
    chunk_spread = chunk_heads * tokens
    maps = maps.reshape(PAIR, side, rows, group_tokens, width)
    same = (jnp.arange(spread)[:, None] // tokens == jnp.arange(spread)[None, :] // tokens).astype(BF16)
    wide = (jnp.arange(spread)[:, None] // tokens == jnp.arange(channels)[None, :] // head_dim).astype(BF16)

    def body(
        slot_ref, len_ref, col_ref, *refs
    ):
        map_refs = refs[:BATCH]
        (
            small_ref, win_ref, state_ref, kern_ref, off_ref, bias_ref, rate_ref, same_ref, wide_ref,
            mat_ref, part_ref, wx_ref, in_ref, last_ref, tail_ref, raw_sc, step_sc, log_sc, weight_sc,
        ) = refs[BATCH : BATCH + 19]
        exts = refs[BATCH + 19 :]
        lane = lax.broadcasted_iota(jnp.int32, (1, spread), 1) % tokens

        @pl.when(pl.program_id(0) == 0)
        def _():
            for s in range(sessions):
                slot = slot_ref[s]
                pair = small_ref[slot // PAIR].astype(F32)
                raw_sc[s : s + 1, :] = jnp.where(slot % PAIR == 0, pair[0:1], pair[1:2])
            valid = (lane < col_ref[...]).astype(F32)
            step = jax.nn.softplus(raw_sc[...] + bias_ref[...]) * valid
            fall = -rate_ref[...] * step
            log = fall
            rest = jnp.where(lane < tokens - 1, pltpu.roll(fall, spread - 1, 1), 0.0)
            hop = 1
            while hop < tokens:
                log = log + jnp.where(lane >= hop, pltpu.roll(log, hop, 1), 0.0)
                rest = rest + jnp.where(lane < tokens - hop, pltpu.roll(rest, spread - hop, 1), 0.0)
                hop *= 2
            step_sc[...] = step
            log_sc[...] = log
            weight_sc[...] = jnp.exp(rest) * step

        token = lax.broadcasted_iota(jnp.int32, (tokens, spread), 0)
        within = lax.broadcasted_iota(jnp.int32, (tokens, spread), 1) % tokens
        diagonal = within == token
        causal = within <= token
        final = lax.broadcasted_iota(jnp.int32, (heads, spread), 1) == (
            lax.broadcasted_iota(jnp.int32, (heads, spread), 0) * tokens + tokens - 1
        )
        for i in range(BATCH):
            c = pl.program_id(0) * BATCH + i
            ext_sc = exts[i]
            step = step_sc[pl.ds(c, 1), :]
            log = log_sc[pl.ds(c, 1), :]
            weight = weight_sc[pl.ds(c, 1), :]
            ext_sc[5:8] = win_ref[i].astype(F32)
            ext_sc[8:] = map_refs[i][0, :, 0].astype(F32).reshape(tokens, width)
            tail_ref[i] = jnp.concatenate(
                [ext_sc[pl.ds(len_ref[c] + 5 + n, 1), :] for n in range(3)], axis=0
            ).astype(BF16)
            conv = convolve(ext_sc, kern_ref[...], off_ref[...], tokens)
            in_high, in_low = halves(conv[:, :state_dim])
            out_high, out_low = halves(conv[:, state_dim:])
            in_ref[i] = jnp.concatenate([in_high, in_low, in_high], axis=0)

            log_all = jnp.broadcast_to(log, (tokens, spread))
            spot = jnp.where(diagonal, log_all, 0.0)
            first = spot.astype(BF16)
            second, third = halves(spot - first.astype(F32))
            own = dot_nn(jnp.concatenate([first, second, third], axis=0), same_ref[...])
            own = own[:tokens] + own[tokens : 2 * tokens] + own[2 * tokens :]
            decay = jnp.where(causal, jnp.exp(jnp.where(causal, own - log_all, 0.0)), 0.0)
            keys = jnp.concatenate([jnp.concatenate([in_high, in_low], axis=1)] * heads, axis=0)
            asks = jnp.concatenate(
                [
                    jnp.concatenate([out_high, out_high], axis=1),
                    jnp.concatenate([out_low, jnp.zeros_like(out_low)], axis=1),
                ],
                axis=0,
            )
            scores = dot_nt(asks, keys)
            scores = scores[:tokens] + scores[tokens:]
            high, low = halves(decay * scores * step)
            for k in range(CHUNKS):
                part = slice(k * chunk_spread, (k + 1) * chunk_spread)
                base = 2 * k * chunk_spread
                mat_ref[i, :, base : base + chunk_spread] = high[:, part]
                mat_ref[i, :, base + chunk_spread : base + 2 * chunk_spread] = low[:, part]

            rise = halves(jnp.where(diagonal, jnp.exp(log_all), 0.0))
            load = halves(jnp.where(diagonal, jnp.broadcast_to(weight, (tokens, spread)), 0.0))
            grown = dot_nn(jnp.concatenate([*rise, *load], axis=0), wide_ref[...])
            wx_ref[i] = grown[2 * tokens : 3 * tokens] + grown[3 * tokens :]
            carried = dot_nt(
                jnp.concatenate([out_high, out_low], axis=0), state_ref[i].reshape(channels, state_dim)
            )
            part_ref[i] = (carried[:tokens] + carried[tokens:]) * (
                grown[:tokens] + grown[tokens : 2 * tokens]
            )
            last = jnp.sum(jnp.where(final, jnp.exp(log), 0.0), axis=1, keepdims=True)
            last_ref[i] = jnp.broadcast_to(last, (heads, 128))

    def whole(*shape):
        return pl.BlockSpec(shape, lambda g, s, n: (0,) * len(shape))

    def at(*shape):
        return pl.BlockSpec((BATCH,) + shape, lambda g, s, n: (g,) + (0,) * len(shape))

    def received(i):
        return pl.BlockSpec(
            (1, side, 1, group_tokens, width),
            lambda g, s, n: (s[g * BATCH + i] % PAIR, 0, s[g * BATCH + i] // PAIR, 0, 0),
        )

    return pl.pallas_call(
        body,
        out_shape=[
            jax.ShapeDtypeStruct((sessions, tokens, 2 * spread), BF16),
            jax.ShapeDtypeStruct((sessions, tokens, channels), F32),
            jax.ShapeDtypeStruct((sessions, tokens, channels), F32),
            jax.ShapeDtypeStruct((sessions, 3 * tokens, state_dim), BF16),
            jax.ShapeDtypeStruct((sessions, heads, 128), F32),
            jax.ShapeDtypeStruct((sessions, 3, width), BF16),
        ],
        grid_spec=pltpu.PrefetchScalarGridSpec(
            num_scalar_prefetch=2,
            grid=(sessions // BATCH,),
            in_specs=[whole(sessions, 1)]
            + [received(i) for i in range(BATCH)]
            + [
                pl.BlockSpec((rows, 8, width), lambda g, s, n: (0, group_tokens // 8, 0)),
                at(3, width),
                at(heads, head_dim, state_dim),
                whole(4, width),
                whole(1, width),
                whole(1, spread),
                whole(1, spread),
                whole(spread, spread),
                whole(spread, channels),
            ],
            out_specs=[
                at(tokens, 2 * spread),
                at(tokens, channels),
                at(tokens, channels),
                at(3 * tokens, state_dim),
                at(heads, 128),
                at(3, width),
            ],
            scratch_shapes=[pltpu.VMEM((sessions, spread), F32)] * 4
            + [pltpu.VMEM((tokens + 8, width), F32)] * BATCH,
        ),
        compiler_params=params(),
        cost_estimate=cost(sessions * (1 << 25), sessions << 19),
        name="prepare",
    )(
        slots, lens, lens_col, *[maps] * BATCH, small, map_window, state, map_kernel, map_bias, bias_row,
        decay_row, same, wide,
    )


def mix(k, slots, lens, fresh, window, prepared, state, kernel, offset, skip, earlier):
    mats, parts, loads, in_maps, lasts = prepared
    slot_total, tokens, width = fresh.shape
    sessions, heads, head_dim, state_dim = state.shape
    chunk_heads = heads // CHUNKS
    chunk_spread = chunk_heads * tokens
    channels = heads * head_dim

    def body(slot_ref, len_ref, *refs):
        new_refs = refs[:BATCH]
        (
            win_ref, mat_ref, part_ref, wx_ref, in_ref, last_ref, state_ref, kern_ref, off_ref, skip_ref,
        ) = refs[BATCH : BATCH + 10]
        y_ref, next_ref, tail_ref, y_sc, sems, *exts = refs[BATCH + 10 + len(earlier) :]
        g = pl.program_id(0)
        turn = g % 2

        def copy(i, group, half):
            return pltpu.make_async_copy(
                y_sc.at[half, i], y_ref.at[slot_ref[group * BATCH + i]], sems.at[half, i]
            )

        @pl.when(g >= 2)
        def _():
            for i in range(BATCH):
                copy(i, g - 2, turn).wait()

        owner = lax.broadcasted_iota(jnp.int32, (chunk_spread, width), 0) // tokens
        lane = lax.broadcasted_iota(jnp.int32, (chunk_spread, width), 1) // head_dim
        own = owner == lane
        zero = jnp.zeros((chunk_spread, width), BF16)
        token = lax.broadcasted_iota(jnp.int32, (tokens, width), 0)
        for i in range(BATCH):
            c = g * BATCH + i
            ext_sc = exts[i]
            ext_sc[5:8] = win_ref[i].astype(F32)
            ext_sc[8:] = new_refs[i][0].astype(F32)
            tail_ref[i] = jnp.concatenate(
                [ext_sc[pl.ds(len_ref[c] + 5 + n, 1), :] for n in range(3)], axis=0
            ).astype(BF16)
            x = convolve(ext_sc, kern_ref[...], off_ref[...], tokens)
            high, low = halves(x)
            tall_high = jnp.where(own, jnp.concatenate([high] * chunk_heads, axis=0), zero)
            tall_low = jnp.where(own, jnp.concatenate([low] * chunk_heads, axis=0), zero)
            mat = mat_ref[i]
            inside = dot_nn(
                jnp.concatenate([mat, mat[:, :chunk_spread]], axis=1),
                jnp.concatenate([tall_high, tall_high, tall_low], axis=0),
            )
            mixed = inside + part_ref[i] + skip_ref[...] * x
            y_sc[turn, i] = jnp.where(token < len_ref[c], mixed, 0.0).astype(BF16)
            copy(i, g, turn).start()
            w_high, w_low = halves(x * wx_ref[i])
            added = dot_tn(jnp.concatenate([w_high, w_high, w_low], axis=0), in_ref[i])
            for h in range(chunk_heads):
                at = k * chunk_heads + h
                next_ref[i, h] = (
                    last_ref[i, at : at + 1, :] * state_ref[i, h].astype(F32)
                    + added[h * head_dim : (h + 1) * head_dim]
                ).astype(BF16)

        @pl.when(g == pl.num_programs(0) - 1)
        def _():
            for i in range(BATCH):
                copy(i, g - 1, 1 - turn).wait()
                copy(i, g, turn).wait()

    def whole(*shape):
        return pl.BlockSpec(shape, lambda g, s, n: (0,) * (len(shape) - 1) + (k,))

    def cut(*shape):
        return pl.BlockSpec((BATCH,) + shape, lambda g, s, n: (g,) + (0,) * (len(shape) - 1) + (k,))

    def at(*shape):
        return pl.BlockSpec((BATCH,) + shape, lambda g, s, n: (g,) + (0,) * len(shape))

    def received(i):
        return pl.BlockSpec((1, tokens, width), lambda g, s, n: (s[g * BATCH + i], 0, 0))

    held = pl.BlockSpec((BATCH, chunk_heads, head_dim, state_dim), lambda g, s, n: (g, k, 0, 0))
    anywhere = pl.BlockSpec(memory_space=pl.ANY)
    operands = [slots, lens, *[fresh] * BATCH, window, mats, parts, loads, in_maps, lasts]
    operands += [state, kernel, offset, skip]
    return pl.pallas_call(
        body,
        out_shape=[
            jax.ShapeDtypeStruct((slot_total, tokens, width), BF16),
            jax.ShapeDtypeStruct(state.shape, BF16),
            jax.ShapeDtypeStruct((sessions, 3, channels), BF16),
        ],
        grid_spec=pltpu.PrefetchScalarGridSpec(
            num_scalar_prefetch=2,
            grid=(sessions // BATCH,),
            in_specs=[received(i) for i in range(BATCH)]
            + [
                cut(3, width),
                cut(tokens, 2 * chunk_spread),
                cut(tokens, width),
                cut(tokens, width),
                at(3 * tokens, state_dim),
                at(heads, 128),
                held,
                whole(4, width),
                whole(1, width),
                whole(1, width),
            ]
            + [anywhere] * len(earlier),
            out_specs=[anywhere, held, cut(3, width)],
            scratch_shapes=[
                pltpu.VMEM((2, BATCH, tokens, width), BF16),
                pltpu.SemaphoreType.DMA((2, BATCH)),
            ]
            + [pltpu.VMEM((tokens + 8, width), F32)] * BATCH,
        ),
        input_output_aliases={len(operands) + i: 1 + i for i in range(len(earlier))},
        compiler_params=params(),
        cost_estimate=cost(sessions * (1 << 24), sessions << 19),
    )(*operands, *earlier)


def gate_rows(k, slots, picks, back, gate, adapters, scale, earlier):
    sessions, tokens, _ = gate.shape
    _, _, width = back.shape
    rank = adapters.shape[1] // 2

    def body(slot_ref, pick_ref, *refs):
        backs, downs = refs[:GROUP], refs[GROUP : 2 * GROUP]
        gate_ref, scale_ref = refs[2 * GROUP : 2 * GROUP + 2]
        sum_ref, gated_ref = refs[-2:]
        for i in range(GROUP):
            gated = backs[i][0].astype(F32) * silu(gate_ref[i].astype(F32))
            gated_ref[i] = gated
            low = dot_nt((gated * scale_ref[...]).astype(BF16), downs[i][0])
            square = jnp.sum(gated * gated, axis=1, keepdims=True)
            both = jnp.concatenate([low, jnp.broadcast_to(square, (tokens, 128 - rank))], axis=1)
            if earlier:
                both = both + refs[2 * GROUP + 2][i * tokens : (i + 1) * tokens]
            sum_ref[i * tokens : (i + 1) * tokens] = both

    def returned(i):
        return pl.BlockSpec((1, tokens, width), lambda g, s, a: (s[g * GROUP + i], 0, 0))

    def chosen(i):
        return pl.BlockSpec((1, rank, width), lambda g, s, a: (a[g * GROUP + i], 0, k))

    sums = pl.BlockSpec((GROUP * tokens, 128), lambda g, s, a: (g, 0))
    return pl.pallas_call(
        body,
        out_shape=[
            jax.ShapeDtypeStruct((sessions * tokens, 128), F32),
            jax.ShapeDtypeStruct((sessions, tokens, width), F32),
        ],
        grid_spec=pltpu.PrefetchScalarGridSpec(
            num_scalar_prefetch=2,
            grid=(sessions // GROUP,),
            in_specs=[returned(i) for i in range(GROUP)]
            + [chosen(i) for i in range(GROUP)]
            + [
                pl.BlockSpec((GROUP, tokens, width), lambda g, s, a: (g, 0, k)),
                pl.BlockSpec((1, width), lambda g, s, a: (0, k)),
            ]
            + [sums] * len(earlier),
            out_specs=[sums, pl.BlockSpec((GROUP, tokens, width), lambda g, s, a: (g, 0, 0))],
        ),
        compiler_params=params(),
        cost_estimate=cost(sessions * (1 << 22), sessions << 18),
    )(slots, picks, *[back] * GROUP, *[adapters] * GROUP, gate, scale, *earlier)


def finish(picks, gated, totals, adapters, scale):
    sessions, tokens, width = gated[0].shape
    channels = width * CHUNKS
    rank = adapters.shape[1] // 2

    def body(pick_ref, *refs):
        ups, rows = refs[:GROUP], refs[GROUP : GROUP + CHUNKS]
        total_ref, scale_ref, out_ref, delta_ref = refs[GROUP + CHUNKS :]
        for i in range(GROUP):
            total = total_ref[i * tokens : (i + 1) * tokens]
            inverse = total[:, rank : rank + 1]
            for k in range(CHUNKS):
                part = slice(k * width, (k + 1) * width)
                out_ref[i, :, part] = (rows[k][i] * inverse * scale_ref[:, part]).astype(BF16)
            delta_ref[i] = dot_nn(total[:, :rank].astype(BF16), ups[i][0]).astype(BF16)

    def chosen(i):
        return pl.BlockSpec((1, rank, channels), lambda g, a: (a[g * GROUP + i], 1, 0))

    out = pl.BlockSpec((GROUP, tokens, channels), lambda g, a: (g, 0, 0))
    return pl.pallas_call(
        body,
        out_shape=[jax.ShapeDtypeStruct((sessions, tokens, channels), BF16)] * 2,
        grid_spec=pltpu.PrefetchScalarGridSpec(
            num_scalar_prefetch=1,
            grid=(sessions // GROUP,),
            in_specs=[chosen(i) for i in range(GROUP)]
            + [pl.BlockSpec((GROUP, tokens, width), lambda g, a: (g, 0, 0))] * CHUNKS
            + [
                pl.BlockSpec((GROUP * tokens, 128), lambda g, a: (g, 0)),
                pl.BlockSpec((1, channels), lambda g, a: (0, 0)),
            ],
            out_specs=[out, out],
        ),
        compiler_params=params(),
        cost_estimate=cost(sessions * (1 << 22), sessions << 18),
        name="finish",
    )(picks, *[adapters] * GROUP, *gated, totals, scale)


def exchange(value, axis, groups=None):
    return lax.all_to_all(
        value, axis, split_axis=0, concat_axis=0, tiled=True, axis_index_groups=groups
    )


def share_all(value, axis, count, groups=None):
    return exchange(
        jnp.broadcast_to(value[None], (count,) + value.shape).reshape((-1,) + value.shape[1:]), axis, groups
    )


def place(spots, blocks):
    count = len(blocks)

    def body(spot_ref, *refs):
        ins, out_ref = refs[:count], refs[count]
        helds, sems = refs[count + 1 : 2 * count + 1], refs[2 * count + 1]
        loads = [pltpu.make_async_copy(ins[i], helds[i], sems.at[0, i]) for i in range(count)]
        for load in loads:
            load.start()
        stores = []
        for i in range(count):
            loads[i].wait()
            stores.append(pltpu.make_async_copy(helds[i], out_ref.at[spot_ref[i]], sems.at[1, i]))
            stores[i].start()
        for store in stores:
            store.wait()

    return pl.pallas_call(
        body,
        out_shape=jax.ShapeDtypeStruct((count,) + blocks[0].shape, blocks[0].dtype),
        in_specs=[pl.BlockSpec(memory_space=pltpu.SMEM)]
        + [pl.BlockSpec(memory_space=pl.ANY)] * count,
        out_specs=pl.BlockSpec(memory_space=pl.ANY),
        scratch_shapes=[pltpu.VMEM(block.shape, block.dtype) for block in blocks]
        + [pltpu.SemaphoreType.DMA((2, count))],
        compiler_params=params(),
        cost_estimate=cost(0, 2 * count * blocks[0].size * 2),
    )(spots, *blocks)


def shifted(value, axis, rings):
    length = len(rings[0])
    held = [value]
    for d in range(1, length):
        pairs = [(ring[i], ring[(i + d) % length]) for ring in rings for i in range(length)]
        held.append(lax.ppermute(value, axis, pairs))
    return held


def origins(position, length):
    return (position - jnp.arange(length, dtype=jnp.int32)) % length


def gather_adapters(block, row, size_z, size_x):
    along_z = [[z * size_x + x for z in range(size_z)] for x in range(size_x)]
    along_x = [[z * size_x + x for x in range(size_x)] for z in range(size_z)]
    column = place(origins(row // size_x, size_z), shifted(block, "row", along_z))
    whole = place(origins(row % size_x, size_x), shifted(column, "row", along_x))
    return whole.reshape((size_z * size_x,) + block.shape)


def shards(
    channel_rows_in,
    gate_rows_in,
    map_input_rows,
    step_size_input,
    channel_kernel_weight,
    map_kernel_weight,
    channel_conv_bias,
    map_kernel_bias,
    step_size_bias,
    head_decay_rate,
    head_skip_weight,
    gated_norm_scale,
    scan_state_cache,
    channel_window_cache,
    map_window_cache,
    adapter_down_weight,
    adapter_up_weight,
    session_slot_index,
    lengths,
    session_adapter_index,
):
    sessions, tokens, channels = channel_rows_in.shape
    heads = step_size_input.shape[1]
    head_dim = channels // heads
    rows = lax.axis_size("row")
    sections = lax.axis_size("section")
    row = lax.axis_index("row")
    section = lax.axis_index("section")
    size_x = 4 if rows >= 32 else 2
    size_z = rows // size_x
    side = sections // PAIR
    group_tokens = tokens // side

    local = jnp.arange(sessions, dtype=jnp.int32)
    mine = lax.dynamic_slice_in_dim(session_slot_index, row * sessions, sessions)
    homes = mine // sessions
    sooner = (homes[None, :] == homes[:, None]) & (local[None, :] < local[:, None])
    serve_slots = homes * PAIR + jnp.sum(sooner.astype(jnp.int32), axis=1)
    here = (session_slot_index // sessions == row).astype(jnp.int32).reshape(rows, sessions)
    ahead = jnp.sum(
        jnp.where(local[None, None, :] < local[None, :, None], here[:, None, :], 0), axis=2
    )
    target = (jnp.arange(rows, dtype=jnp.int32)[:, None] * PAIR + ahead).reshape(-1)
    match = session_slot_index[None, :] == (row * sessions + local)[:, None]
    home_slots = jnp.sum(jnp.where(match, target[None, :], 0), axis=1)
    home_lens = jnp.sum(jnp.where(match, lengths[None, :], 0), axis=1)
    adapter = lax.dynamic_slice_in_dim(session_adapter_index, row * sessions, sessions)
    picks = adapter % size_x * size_z + adapter // size_x

    map_slice = lax.dynamic_slice_in_dim(
        map_input_rows, section % side * group_tokens, group_tokens, axis=1
    )
    step_rows = step_size_input.reshape(sessions, heads * tokens).astype(F32)
    small = pack_small(serve_slots, (section // side).reshape(1), map_slice, step_rows)
    small = exchange(small, "row")
    sent = pack_channels(serve_slots, channel_rows_in, rows * PAIR)
    fresh = []
    for k in range(CHUNKS):
        fresh.append(exchange(sent[k], "row"))
    block = jnp.concatenate([adapter_down_weight[0], adapter_up_weight[0]], axis=0)
    adapters = gather_adapters(block, row, size_z, size_x)
    maps = place(
        origins(section, sections),
        shifted(small[:, :group_tokens], "section", [list(range(sections))]),
    )
    *prepared, map_window_next = prepare(
        home_slots,
        home_lens,
        home_lens[:, None],
        maps,
        small,
        map_window_cache,
        scan_state_cache,
        map_kernel_weight,
        map_kernel_bias[None],
        jnp.repeat(step_size_bias, tokens)[None],
        jnp.repeat(head_decay_rate, tokens)[None],
    )
    skip = jnp.repeat(head_skip_weight, head_dim)[None]
    scale = gated_norm_scale[None]
    back = []
    carried = []
    for k in range(CHUNKS):
        mixed, *carried = mix(
            k,
            home_slots,
            home_lens,
            fresh[k],
            channel_window_cache,
            prepared,
            scan_state_cache,
            channel_kernel_weight,
            channel_conv_bias[None],
            skip,
            carried,
        )
        back.append(exchange(mixed, "row"))
    scan_state_next, channel_window_next = carried
    sums = []
    gated = []
    for k in range(CHUNKS):
        total, part = gate_rows(k, serve_slots, picks, back[k], gate_rows_in, adapters, scale, sums)
        sums = [total]
        gated.append(part)
    rank = adapter_down_weight.shape[1]
    share = exchange(sums[0], "section")
    share = jnp.sum(share.reshape(sections, -1, 128), axis=0)
    inverse = lax.rsqrt(share[:, rank:] / (channels * sections) + NORM_EPS)
    share = jnp.concatenate([share[:, :rank] * inverse[:, :1], inverse], axis=1)
    totals = share_all(share, "section", sections)
    mixer_output_rows, adapter_delta = finish(picks, gated, totals, adapters, scale)
    return (mixer_output_rows, adapter_delta, scan_state_next, channel_window_next, map_window_next)


def solution(mesh):
    split = P("row", None, "section")
    return jax.shard_map(
        shards,
        mesh=mesh,
        in_specs=(
            split,
            split,
            P("row", None, None),
            P("row", "section", None),
            P(None, "section"),
            P(),
            P("section"),
            P(),
            P("section"),
            P("section"),
            P("section"),
            P("section"),
            P("row", "section", None, None),
            split,
            P("row", None, None),
            split,
            split,
            P(),
            P(),
            P(),
        ),
        out_specs=(
            split,
            split,
            P("row", "section", None, None),
            split,
            P("row", None, None),
        ),
        check_vma=False,
    )
```

time: 670 us -> 318 us (0.47)
  waiting for transfers between devices: 338 us -> 110 us
  matrix products: 86.7 us -> 0 us
  local copies, waits for them, and re-layouts: 82.4 us -> 13.4 us
  Pallas kernels: 0 us -> 67 us
  other arithmetic: 27.2 us -> 8.53 us
  between operations: 14.9 us -> 1.14 us
    all_gather x2 -> x0, waiting for transfers between devices: 180 us -> none  [the longest x1 97.4 us: shards(): lax.all_gather(adapter_down_weight, 'row', axis=0, tiled=True)]
    all_to_all x6 -> x5, waiting for transfers between devices: 156 us -> 35.9 us  [exchange(): lax.all_to_all(value, axis, split_axis=0, concat_axis=0, tiled=True, axis...]
    dot_general x22 -> x0, matrix products: 86.7 us -> none  [the longest x12 28.4 us: pick_rows(): jnp.dot(onehot.astype(source_rows.dtype), source_rows, preferred_element_...]
    ppermute x0 -> x17, waiting for transfers between devices: none -> 73.7 us  [shifted(): held.append(lax.ppermute(value, axis, pairs))]
    pallas_call x0 -> x11, Pallas kernels: none -> 67 us  [the longest x2 20.1 us: mix(): pl.pallas_call(body, out_shape=[jax.ShapeDtypeStruct((slot_total, tokens,...]
    psum x2 -> x0, blocking collectives: 53 us -> none  [the longest x1 29.2 us: shards(): low_total = lax.psum(low_part, 'section').astype(jnp.bfloat16)]
    all_to_all x0 -> x2, blocking collectives: none -> 48.5 us  [exchange(): lax.all_to_all(value, axis, split_axis=0, concat_axis=0, tiled=True, axis...]
    all_to_all x12 -> x0, local copies, waits for them, and re-layouts: 44.6 us -> none  [the longest x2 20.7 us: shards(): lax.all_to_all(pick_rows(scan_state_cache.reshape(local_sess, -1), home_t...]
  transfers between devices with their start and end apart: 8 -> 22, of which waited for: 4 -> 10; matrix products, arithmetic and copies ran while one was open for 20% -> 4% of each run, Pallas kernels for 0% -> 16%
where the time goes in v1:
time: 318 us; the launch traced here: 315 us
  waiting for transfers between devices  110 us (35%)
  Pallas kernels  67 us (21%)
  starting transfers between devices  66.7 us (21%)
  blocking collectives  48.5 us (15%)
  local copies, waits for them, and re-layouts  13.4 us (4%)
  other arithmetic  8.53 us (3%)
    ppermute x17, waiting for transfers between devices, shifted(): held.append(lax.ppermute(value, axis, pairs))  73.7 us
    all_to_all x2, blocking collectives, exchange(): lax.all_to_all(value, axis, split_axis=0, concat_axis=0, tiled=True, axis...  48.5 us
    all_to_all x5, starting transfers between devices, exchange(): lax.all_to_all(value, axis, split_axis=0, concat_axis=0, tiled=True, axis...  36.1 us
    all_to_all x5, waiting for transfers between devices, exchange(): lax.all_to_all(value, axis, split_axis=0, concat_axis=0, tiled=True, axis...  35.9 us
    ppermute x17, starting transfers between devices, shifted(): held.append(lax.ppermute(value, axis, pairs))  30.7 us
    pallas_call x2, Pallas kernels, mix(): pl.pallas_call(body, out_shape=[jax.ShapeDtypeStruct((slot_total, tokens,...  20.1 us
    pallas_call x2, Pallas kernels, gate_rows(): pl.pallas_call(body, out_shape=[jax.ShapeDtypeStruct((sessions * tokens,...  13.9 us
    pallas_call x1, Pallas kernels, prepare(): pl.pallas_call(body, out_shape=[jax.ShapeDtypeStruct((sessions, tokens, 2...  11.5 us
  transfers between devices with their start and end apart: 22, of which 10 were waited for; matrix products, arithmetic and copies ran while one was open for 4% of the time, Pallas kernels for 16%

profile of v1, /device:TPU:2, one launch (start us, length us, event | category | flops | bytes accessed | tf_op | source)
XLA Modules:
  0.0 314.9 jit_solution(6451409402592116622)
XLA Ops:
  7.3 11.6 %all-to-all-start.1 = ((bf16[32,16,256]{2,1,0:T(8,128)(2,1)}), bf16[32,16,256]{2,1,0:T(8,128)(2,1)S(1)}, u32[]{:S(2)}, u32[]{:S(2)}) async-start(bf16[32,16,256]{2,1,0:T(8,128)(2,1)} %pack_small.1), calls=%async_computation.1 | async-start | bytes 524288 | tf_op jit(solution)/shard_map/all_to_all | solution.py:501
  21.7 8.4 %all-to-all-done.1.refs_4_ = bf16[32,16,256]{2,1,0:T(8,128)(2,1)S(1)} async-done(((bf16[32,16,256]{2,1,0:T(8,128)(2,1)}), bf16[32,16,256]{2,1,0:T(8,128)(2,1)S(1)}, u32[]{:S(2)}, u32[]{:S(2)}) %all-to-all-start.1) | async-done | bytes 262176 | tf_op jit(solution)/shard_map/all_to_all | solution.py:501
  30.2 33.0 %all_to_all.42.refs_0_.refs_1_.refs_2_.refs_3_ = bf16[64,32,256]{2,1,0:T(8,128)(2,1)} all-to-all(bf16[64,32,256]{2,1,0:T(8,128)(2,1)} %get-tuple-element.25), channel_id=1, replica_groups=mesh['section'=8,'row'=32] {'row'}, dimensions={0} | all-to-all | bytes 2097152 | tf_op jit(solution)/shard_map/all_to_all | solution.py:501
  63.1 5.6 %all-to-all-start.3 = ((bf16[64,32,256]{2,1,0:T(8,128)(2,1)}), bf16[64,32,256]{2,1,0:T(8,128)(2,1)S(1)}, u32[]{:S(2)}, u32[]{:S(2)}) async-start(bf16[64,32,256]{2,1,0:T(8,128)(2,1)} %get-tuple-element.33), calls=%async_computation.3 | async-start | bytes 2097152 | tf_op jit(solution)/shard_map/all_to_all | solution.py:501
  91.5 11.5 %prepare.1 = (bf16[32,32,512]{2,1,0:T(8,128)(2,1)}, f32[32,32,512]{2,1,0:T(8,128)}, f32[32,32,512]{2,1,0:T(8,128)}, bf16[32,96,128]{2,1,0:T(8,128)(2,1)}, f32[32...) custom-call(s32[32]{0:T(128)} %get-tuple-element.66.slot_ref, s32[32]{0:T(128)} %copy-done.26, s32[32,1]{1,0:T(8,128)} %copy.46.col_ref, ...), custom_call_target="tpu_custom_call" | custom-call | flops 1073741824 | bytes 16777216 | tf_op jit(solution)/shard_map/prepare/pallas_call | solution.py:245
  103.0 10.0 %shard_map.230 = (bf16[64,32,256]{2,1,0:T(8,128)(2,1)}, bf16[32,8,64,128]{3,2,1,0:T(8,128)(2,1)}, bf16[32,3,512]{2,1,0:T(4,128)(2,1)}) custom-call(s32[32]{0:T(128)} %get-tuple-element.66.slot_ref, s32[32]{0:T(128)} %copy-done.26, bf16[64,32,256]{2,1,0:T(8,128)(2,1)} %all_to_all.42.refs_0_.refs_1_.refs_2_.refs_3_, ...), custom_call_target="tpu_custom_call" | custom-call | flops 536870912 | bytes 16777216 | tf_op jit(solution)/shard_map/pallas_call | solution.py:374
  114.0 9.8 %all-to-all-start.2 = ((bf16[64,32,256]{2,1,0:T(8,128)(2,1)}), bf16[64,32,256]{2,1,0:T(8,128)(2,1)S(1)}, u32[]{:S(2)}, u32[]{:S(2)}) async-start(bf16[64,32,256]{2,1,0:T(8,128)(2,1)} %get-tuple-element.31), calls=%async_computation.2 | async-start | bytes 2097152 | tf_op jit(solution)/shard_map/all_to_all | solution.py:501
  123.8 10.1 %shard_map.232 = (bf16[64,32,256]{2,1,0:T(8,128)(2,1)}, bf16[32,8,64,128]{3,2,1,0:T(8,128)(2,1)}, bf16[32,3,512]{2,1,0:T(4,128)(2,1)}) custom-call(s32[32]{0:T(128)} %get-tuple-element.66.slot_ref, s32[32]{0:T(128)} %copy-done.26, bf16[64,32,256]{2,1,0:T(8,128)(2,1)} %copy-done.2, ...), custom_call_target="tpu_custom_call", output_to_operand_aliasing={{1}: (16, {}), {2}: (17, {})} | custom-call | flops 536870912 | bytes 16777216 | tf_op jit(solution)/shard_map/pallas_call | solution.py:374
  133.9 18.5 %all-to-all-done.2.refs_0_.refs_1_.refs_2_.refs_3_ = bf16[64,32,256]{2,1,0:T(8,128)(2,1)S(1)} async-done(((bf16[64,32,256]{2,1,0:T(8,128)(2,1)}), bf16[64,32,256]{2,1,0:T(8,128)(2,1)S(1)}, u32[]{:S(2)}, u32[]{:S(2)}) %all-to-all-start.2) | async-done | bytes 1048608 | tf_op jit(solution)/shard_map/all_to_all | solution.py:501
  152.5 5.6 %all-to-all-start.4 = ((bf16[64,32,256]{2,1,0:T(8,128)(2,1)}), bf16[64,32,256]{2,1,0:T(8,128)(2,1)}, u32[]{:S(2)}, u32[]{:S(2)}) async-start(bf16[64,32,256]{2,1,0:T(8,128)(2,1)} %get-tuple-element.36), calls=%async_computation.4 | async-start | bytes 2097152 | tf_op jit(solution)/shard_map/all_to_all | solution.py:501
  169.8 17.8 %collective-permute-done.refs_1_ = bf16[128,512]{1,0:T(8,128)(2,1)S(1)} collective-permute-done((bf16[128,512]{1,0:T(8,128)(2,1)S(1)}, bf16[128,512]{1,0:T(8,128)(2,1)S(1)}, u32[]{:S(2)}, u32[]{:S(2)}) %collective-permute-start) | collective-permute-done | bytes 131104 | tf_op jit(solution)/shard_map/ppermute | solution.py:547
  190.2 5.2 %collective-permute-done.1.refs_2_ = bf16[128,512]{1,0:T(8,128)(2,1)S(1)} collective-permute-done((bf16[128,512]{1,0:T(8,128)(2,1)S(1)}, bf16[128,512]{1,0:T(8,128)(2,1)S(1)}, u32[]{:S(2)}, u32[]{:S(2)}) %collective-permute-start.1) | collective-permute-done | bytes 131104 | tf_op jit(solution)/shard_map/ppermute | solution.py:547
  197.1 3.5 %collective-permute-done.2.refs_3_ = bf16[128,512]{1,0:T(8,128)(2,1)S(1)} collective-permute-done((bf16[128,512]{1,0:T(8,128)(2,1)S(1)}, bf16[128,512]{1,0:T(8,128)(2,1)S(1)}, u32[]{:S(2)}, u32[]{:S(2)}) %collective-permute-start.2) | collective-permute-done | bytes 131104 | tf_op jit(solution)/shard_map/ppermute | solution.py:547
  200.7 5.3 %collective-permute-done.3.refs_4_ = bf16[128,512]{1,0:T(8,128)(2,1)S(1)} collective-permute-done((bf16[128,512]{1,0:T(8,128)(2,1)S(1)}, bf16[128,512]{1,0:T(8,128)(2,1)S(1)}, u32[]{:S(2)}, u32[]{:S(2)}) %collective-permute-start.3) | collective-permute-done | bytes 131104 | tf_op jit(solution)/shard_map/ppermute | solution.py:547
  207.4 2.8 shard_map.227.refs_0_
  216.7 19.9 %collective-permute-done.7.refs_1_ = bf16[8,128,512]{2,1,0:T(8,128)(2,1)} collective-permute-done((bf16[8,128,512]{2,1,0:T(8,128)(2,1)}, bf16[8,128,512]{2,1,0:T(8,128)(2,1)}, u32[]{:S(2)}, u32[]{:S(2)}) %collective-permute-start.7) | collective-permute-done | bytes 1048608 | tf_op jit(solution)/shard_map/ppermute | solution.py:547
  239.1 19.3 %collective-permute-done.9.refs_3_ = bf16[8,128,512]{2,1,0:T(8,128)(2,1)} collective-permute-done((bf16[8,128,512]{2,1,0:T(8,128)(2,1)}, bf16[8,128,512]{2,1,0:T(8,128)(2,1)}, u32[]{:S(2)}, u32[]{:S(2)}) %collective-permute-start.9) | collective-permute-done | bytes 1048608 | tf_op jit(solution)/shard_map/ppermute | solution.py:547
  258.4 4.0 %shard_map.228 = bf16[4,8,128,512]{3,2,1,0:T(8,128)(2,1)} custom-call(s32[4]{0:T(128)} %and_select_fusion.4.spot_ref, bf16[8,128,512]{2,1,0:T(8,128)(2,1)} %shard_map.227.refs_0_, bf16[8,128,512]{2,1,0:T(8,128)(2,1)} %collective-permute-done.7.refs_1_, bf16[8,128,512]{2,1,0:T(8,128)(2,1)} %collective-permute-done.8.refs_2_, ...), custom_call_target="tpu_custom_call" | custom-call | bytes 8388608 | tf_op jit(solution)/shard_map/pallas_call | solution.py:529
  262.4 6.8 %shard_map.231 = (f32[1024,128]{1,0:T(8,128)}, f32[32,32,256]{2,1,0:T(8,128)}) custom-call(s32[32]{0:T(128)} %multiply_add_fusion.slot_ref, s32[32]{0:T(128)} %fusion.12.pick_ref, bf16[64,32,256]{2,1,0:T(8,128)(2,1)} %copy-done.1, bf16[64,32,256]{2,1,0:T(8,128)(2,1)} %copy-done.1, bf16[64,32,256]{2,1,0:T(8,128)(2,1)} %copy-done.1, ...), custom_call_target="tpu_custom_call" | custom-call | flops 134217728 | bytes 8388608 | tf_op jit(solution)/shard_map/pallas_call | solution.py:437
  269.2 7.2 %shard_map.233 = (f32[1024,128]{1,0:T(8,128)}, f32[32,32,256]{2,1,0:T(8,128)}) custom-call(s32[32]{0:T(128)} %multiply_add_fusion.slot_ref, s32[32]{0:T(128)} %fusion.12.pick_ref, bf16[64,32,256]{2,1,0:T(8,128)(2,1)} %all-to-all-done.4.refs_0_.refs_1_.refs_2_.refs_3_, bf16[64,32,256]{2,1,0:T(8,128)(2,1)} %all-to-all-done.4.refs_0_.refs_1_.refs_2_.refs_3_, ...), custom_call_target="tpu_custom_call" | custom-call | flops 134217728 | bytes 8388608 | tf_op jit(solution)/shard_map/pallas_call | solution.py:437
  276.4 15.5 %all_to_all.43 = f32[8,128,128]{2,1,0:T(8,128)S(1)} all-to-all(f32[8,128,128]{2,1,0:T(8,128)} %bitcast.28), channel_id=1, replica_groups=mesh['section'=8,'row'=32] {'section'}, dimensions={0} | all-to-all | bytes 1048576 | tf_op jit(solution)/shard_map/all_to_all | solution.py:501
  293.2 3.5 %all-to-all-start.6 = ((f32[8,128,128]{2,1,0:T(8,128)}), f32[8,128,128]{2,1,0:T(8,128)S(1)}, u32[]{:S(2)}, u32[]{:S(2)}) async-start(f32[8,128,128]{2,1,0:T(8,128)} %broadcast_in_dim.100), calls=%async_computation.6 | async-start | bytes 1048576 | tf_op jit(solution)/shard_map/all_to_all | solution.py:501
  298.0 8.9 %all-to-all-done.6 = f32[8,128,128]{2,1,0:T(8,128)S(1)} async-done(((f32[8,128,128]{2,1,0:T(8,128)}), f32[8,128,128]{2,1,0:T(8,128)S(1)}, u32[]{:S(2)}, u32[]{:S(2)}) %all-to-all-start.6) | async-done | bytes 524320 | tf_op jit(solution)/shard_map/all_to_all | solution.py:501
  307.8 7.2 %finish.1 = (bf16[32,32,512]{2,1,0:T(8,128)(2,1)}, bf16[32,32,512]{2,1,0:T(8,128)(2,1)}) custom-call(s32[32]{0:T(128)} %fusion.12.pick_ref, bf16[32,128,512]{2,1,0:T(8,128)(2,1)} %bitcast.19, bf16[32,128,512]{2,1,0:T(8,128)(2,1)} %bitcast.20, bf16[32,128,512]{2,1,0:T(8,128)(2,1)} %bitcast.21, bf16[32,128,512]{2,1,0:T(8,128)(2,1)} %bitcast.22, ...), custom_call_target="tpu_custom_call" | custom-call | flops 134217728 | bytes 8388608 | tf_op jit(solution)/shard_map/finish/pallas_call | solution.py:480
  (136 shorter events, 62.8 us)
Async XLA Ops:
  0.7 83.2 %copy-start.28 = (f32[8]{0:T(128)S(1)}, f32[8]{0:T(128)}, u32[]{:S(2)}) copy-start(f32[8]{0:T(128)} %param.28) | copy-start | bytes 100
  7.3 22.8 %all-to-all-start.1 = ((bf16[32,16,256]{2,1,0:T(8,128)(2,1)}), bf16[32,16,256]{2,1,0:T(8,128)(2,1)S(1)}, u32[]{:S(2)}, u32[]{:S(2)}) async-start(bf16[32,16,256]{2,1,0:T(8,128)(2,1)} %pack_small.1), calls=%async_computation.1 | async-start | bytes 524288 | tf_op jit(solution)/shard_map/all_to_all | solution.py:501
  63.1 49.9 %all-to-all-start.3 = ((bf16[64,32,256]{2,1,0:T(8,128)(2,1)}), bf16[64,32,256]{2,1,0:T(8,128)(2,1)S(1)}, u32[]{:S(2)}, u32[]{:S(2)}) async-start(bf16[64,32,256]{2,1,0:T(8,128)(2,1)} %get-tuple-element.33), calls=%async_computation.3 | async-start | bytes 2097152 | tf_op jit(solution)/shard_map/all_to_all | solution.py:501
  71.1 7.7 %collective-permute-start.10 = (bf16[32,8,256]{2,1,0:T(8,128)(2,1)S(1)}, bf16[32,8,256]{2,1,0:T(8,128)(2,1)S(1)}, u32[]{:S(2)}, u32[]{:S(2)}) collective-permute-start(bf16[32,8,256]{2,1,0:T(8,128)(2,1)S(1)} %slice.16.refs_0_), channel_id=1, source_target_pairs={{0,32},{32,64},{64,96},{96,128},{128,160},{160,192},{192,224},{224... | collective-permute-start | bytes 393224 | tf_op jit(solution)/shard_map/ppermute | solution.py:547
  71.1 9.0 %collective-permute-start.11 = (bf16[32,8,256]{2,1,0:T(8,128)(2,1)S(1)}, bf16[32,8,256]{2,1,0:T(8,128)(2,1)S(1)}, u32[]{:S(2)}, u32[]{:S(2)}) collective-permute-start(bf16[32,8,256]{2,1,0:T(8,128)(2,1)S(1)} %slice.16.refs_0_), channel_id=1, source_target_pairs={{0,64},{32,96},{64,128},{96,160},{128,192},{160,224},{192,0},{224,... | collective-permute-start | bytes 393224 | tf_op jit(solution)/shard_map/ppermute | solution.py:547
  72.9 14.4 %collective-permute-start.12 = (bf16[32,8,256]{2,1,0:T(8,128)(2,1)S(1)}, bf16[32,8,256]{2,1,0:T(8,128)(2,1)S(1)}, u32[]{:S(2)}, u32[]{:S(2)}) collective-permute-start(bf16[32,8,256]{2,1,0:T(8,128)(2,1)S(1)} %slice.16.refs_0_), channel_id=1, source_target_pairs={{0,96},{32,128},{64,160},{96,192},{128,224},{160,0},{192,32},{224,... | collective-permute-start | bytes 393224 | tf_op jit(solution)/shard_map/ppermute | solution.py:547
  75.1 12.2 %collective-permute-start.13 = (bf16[32,8,256]{2,1,0:T(8,128)(2,1)S(1)}, bf16[32,8,256]{2,1,0:T(8,128)(2,1)S(1)}, u32[]{:S(2)}, u32[]{:S(2)}) collective-permute-start(bf16[32,8,256]{2,1,0:T(8,128)(2,1)S(1)} %slice.16.refs_0_), channel_id=1, source_target_pairs={{0,128},{32,160},{64,192},{96,224},{128,0},{160,32},{192,64},{224,... | collective-permute-start | bytes 393224 | tf_op jit(solution)/shard_map/ppermute | solution.py:547
  77.0 10.4 %collective-permute-start.14 = (bf16[32,8,256]{2,1,0:T(8,128)(2,1)S(1)}, bf16[32,8,256]{2,1,0:T(8,128)(2,1)S(1)}, u32[]{:S(2)}, u32[]{:S(2)}) collective-permute-start(bf16[32,8,256]{2,1,0:T(8,128)(2,1)S(1)} %slice.16.refs_0_), channel_id=1, source_target_pairs={{0,160},{32,192},{64,224},{96,0},{128,32},{160,64},{192,96},{224,1... | collective-permute-start | bytes 393224 | tf_op jit(solution)/shard_map/ppermute | solution.py:547
  78.8 8.6 %collective-permute-start.15 = (bf16[32,8,256]{2,1,0:T(8,128)(2,1)S(1)}, bf16[32,8,256]{2,1,0:T(8,128)(2,1)S(1)}, u32[]{:S(2)}, u32[]{:S(2)}) collective-permute-start(bf16[32,8,256]{2,1,0:T(8,128)(2,1)S(1)} %slice.16.refs_0_), channel_id=1, source_target_pairs={{0,192},{32,224},{64,0},{96,32},{128,64},{160,96},{192,128},{224,1... | collective-permute-start | bytes 393224 | tf_op jit(solution)/shard_map/ppermute | solution.py:547
  80.1 8.6 %collective-permute-start.16 = (bf16[32,8,256]{2,1,0:T(8,128)(2,1)S(1)}, bf16[32,8,256]{2,1,0:T(8,128)(2,1)}, u32[]{:S(2)}, u32[]{:S(2)}) collective-permute-start(bf16[32,8,256]{2,1,0:T(8,128)(2,1)S(1)} %slice.16.refs_0_), channel_id=1, source_target_pairs={{0,224},{32,0},{64,32},{96,64},{128,96},{160,128},{192,160},{224,1... | collective-permute-start | bytes 393224 | tf_op jit(solution)/shard_map/ppermute | solution.py:547
  114.0 38.5 %all-to-all-start.2 = ((bf16[64,32,256]{2,1,0:T(8,128)(2,1)}), bf16[64,32,256]{2,1,0:T(8,128)(2,1)S(1)}, u32[]{:S(2)}, u32[]{:S(2)}) async-start(bf16[64,32,256]{2,1,0:T(8,128)(2,1)} %get-tuple-element.31), calls=%async_computation.2 | async-start | bytes 2097152 | tf_op jit(solution)/shard_map/all_to_all | solution.py:501
  152.5 110.0 %copy-start.1 = (bf16[64,32,256]{2,1,0:T(8,128)(2,1)}, bf16[64,32,256]{2,1,0:T(8,128)(2,1)S(1)}, u32[]{:S(2)}) copy-start(bf16[64,32,256]{2,1,0:T(8,128)(2,1)S(1)} %all-to-all-done.2.refs_0_.refs_1_.refs_2_.refs_3_) | copy-start | bytes 3145732
  152.5 116.7 %all-to-all-start.4 = ((bf16[64,32,256]{2,1,0:T(8,128)(2,1)}), bf16[64,32,256]{2,1,0:T(8,128)(2,1)}, u32[]{:S(2)}, u32[]{:S(2)}) async-start(bf16[64,32,256]{2,1,0:T(8,128)(2,1)} %get-tuple-element.36), calls=%async_computation.4 | async-start | bytes 2097152 | tf_op jit(solution)/shard_map/all_to_all | solution.py:501
  158.1 29.5 %collective-permute-start = (bf16[128,512]{1,0:T(8,128)(2,1)S(1)}, bf16[128,512]{1,0:T(8,128)(2,1)S(1)}, u32[]{:S(2)}, u32[]{:S(2)}) collective-permute-start(bf16[128,512]{1,0:T(8,128)(2,1)S(1)} %pad_maximum_fusion.refs_0_), channel_id=1, source_target_pairs={{0,4},{4,8},{8,12},{12,16},{16,20},{20,24},{24,28},{28,0},{1,5},{5... | collective-permute-start | bytes 393224 | tf_op jit(solution)/shard_map/ppermute | solution.py:547
  159.7 35.7 %collective-permute-start.1 = (bf16[128,512]{1,0:T(8,128)(2,1)S(1)}, bf16[128,512]{1,0:T(8,128)(2,1)S(1)}, u32[]{:S(2)}, u32[]{:S(2)}) collective-permute-start(bf16[128,512]{1,0:T(8,128)(2,1)S(1)} %pad_maximum_fusion.refs_0_), channel_id=1, source_target_pairs={{0,8},{4,12},{8,16},{12,20},{16,24},{20,28},{24,0},{28,4},{1,9},{5... | collective-permute-start | bytes 393224 | tf_op jit(solution)/shard_map/ppermute | solution.py:547
  162.1 38.6 %collective-permute-start.2 = (bf16[128,512]{1,0:T(8,128)(2,1)S(1)}, bf16[128,512]{1,0:T(8,128)(2,1)S(1)}, u32[]{:S(2)}, u32[]{:S(2)}) collective-permute-start(bf16[128,512]{1,0:T(8,128)(2,1)S(1)} %pad_maximum_fusion.refs_0_), channel_id=1, source_target_pairs={{0,12},{4,16},{8,20},{12,24},{16,28},{20,0},{24,4},{28,8},{1,13},{... | collective-permute-start | bytes 393224 | tf_op jit(solution)/shard_map/ppermute | solution.py:547
  164.8 41.2 %collective-permute-start.3 = (bf16[128,512]{1,0:T(8,128)(2,1)S(1)}, bf16[128,512]{1,0:T(8,128)(2,1)S(1)}, u32[]{:S(2)}, u32[]{:S(2)}) collective-permute-start(bf16[128,512]{1,0:T(8,128)(2,1)S(1)} %pad_maximum_fusion.refs_0_), channel_id=1, source_target_pairs={{0,16},{4,20},{8,24},{12,28},{16,0},{20,4},{24,8},{28,12},{1,17},{... | collective-permute-start | bytes 393224 | tf_op jit(solution)/shard_map/ppermute | solution.py:547
  167.1 38.9 %collective-permute-start.4 = (bf16[128,512]{1,0:T(8,128)(2,1)S(1)}, bf16[128,512]{1,0:T(8,128)(2,1)S(1)}, u32[]{:S(2)}, u32[]{:S(2)}) collective-permute-start(bf16[128,512]{1,0:T(8,128)(2,1)S(1)} %pad_maximum_fusion.refs_0_), channel_id=1, source_target_pairs={{0,20},{4,24},{8,28},{12,0},{16,4},{20,8},{24,12},{28,16},{1,21},{... | collective-permute-start | bytes 393224 | tf_op jit(solution)/shard_map/ppermute | solution.py:547
  187.6 18.4 %collective-permute-start.5 = (bf16[128,512]{1,0:T(8,128)(2,1)S(1)}, bf16[128,512]{1,0:T(8,128)(2,1)S(1)}, u32[]{:S(2)}, u32[]{:S(2)}) collective-permute-start(bf16[128,512]{1,0:T(8,128)(2,1)S(1)} %pad_maximum_fusion.refs_0_), channel_id=1, source_target_pairs={{0,24},{4,28},{8,0},{12,4},{16,8},{20,12},{24,16},{28,20},{1,25},{... | collective-permute-start | bytes 393224 | tf_op jit(solution)/shard_map/ppermute | solution.py:547
  195.4 12.0 %collective-permute-start.6 = (bf16[128,512]{1,0:T(8,128)(2,1)S(1)}, bf16[128,512]{1,0:T(8,128)(2,1)}, u32[]{:S(2)}, u32[]{:S(2)}) collective-permute-start(bf16[128,512]{1,0:T(8,128)(2,1)S(1)} %pad_maximum_fusion.refs_0_), channel_id=1, source_target_pairs={{0,28},{4,0},{8,4},{12,8},{16,12},{20,16},{24,20},{28,24},{1,29},{... | collective-permute-start | bytes 393224 | tf_op jit(solution)/shard_map/ppermute | solution.py:547
  210.1 26.4 %collective-permute-start.7 = (bf16[8,128,512]{2,1,0:T(8,128)(2,1)}, bf16[8,128,512]{2,1,0:T(8,128)(2,1)}, u32[]{:S(2)}, u32[]{:S(2)}) collective-permute-start(bf16[8,128,512]{2,1,0:T(8,128)(2,1)} %shard_map.227.refs_0_), channel_id=1, source_target_pairs={{0,1},{1,2},{2,3},{3,0},{4,5},{5,6},{6,7},{7,4},{8,9},{9,10},{10,1... | collective-permute-start | bytes 3145736 | tf_op jit(solution)/shard_map/ppermute | solution.py:547
  211.3 27.9 %collective-permute-start.8 = (bf16[8,128,512]{2,1,0:T(8,128)(2,1)}, bf16[8,128,512]{2,1,0:T(8,128)(2,1)}, u32[]{:S(2)}, u32[]{:S(2)}) collective-permute-start(bf16[8,128,512]{2,1,0:T(8,128)(2,1)} %shard_map.227.refs_0_), channel_id=1, source_target_pairs={{0,2},{1,3},{2,0},{3,1},{4,6},{5,7},{6,4},{7,5},{8,10},{9,11},{10,... | collective-permute-start | bytes 3145736 | tf_op jit(solution)/shard_map/ppermute | solution.py:547
  212.7 45.7 %collective-permute-start.9 = (bf16[8,128,512]{2,1,0:T(8,128)(2,1)}, bf16[8,128,512]{2,1,0:T(8,128)(2,1)}, u32[]{:S(2)}, u32[]{:S(2)}) collective-permute-start(bf16[8,128,512]{2,1,0:T(8,128)(2,1)} %shard_map.227.refs_0_), channel_id=1, source_target_pairs={{0,3},{1,0},{2,1},{3,2},{4,7},{5,4},{6,5},{7,6},{8,11},{9,8},{10,9... | collective-permute-start | bytes 3145736 | tf_op jit(solution)/shard_map/ppermute | solution.py:547
  293.2 13.7 %all-to-all-start.6 = ((f32[8,128,128]{2,1,0:T(8,128)}), f32[8,128,128]{2,1,0:T(8,128)S(1)}, u32[]{:S(2)}, u32[]{:S(2)}) async-start(f32[8,128,128]{2,1,0:T(8,128)} %broadcast_in_dim.100), calls=%async_computation.6 | async-start | bytes 1048576 | tf_op jit(solution)/shard_map/all_to_all | solution.py:501
  (29 other events, 747.3 us)
